TPU v7x, 512 devices: a whole 4x8x8 slice. The times are simulated.
512 devices in a mesh: cells: 32 (over y, x), genes: 16 (over z, core).
Axes of the slice: x: 4, y: 8, z: 8, core: 2. Of those that a mesh axis runs over, the one named last changes fastest.
Arguments:
- counts: int32 [32768, 4096], P('cells', 'genes'), may hold values from 0 to 128, as said below
- batch: int32 [32768, 1], P(('cells', 'genes')), may hold values from 0 to 63
- seeds: int32 [32768, 1], P(('cells', 'genes')), may hold values from 0 to 1023
- loadings: bfloat16 [4096, 256], P('genes'), may hold values from -0.09375 to 0.09375
Outputs:
- embedding: float32 [32768, 256], P(('cells', 'genes'))
- assign: float32 [32768, 1024], P(('cells', 'genes'))
- centroids: bfloat16 [1024, 256], replicated
Inputs may be any that keep to these rules, and one draw needn't show every extreme that they name: counts[i, g] >= 1 wherever g mod 64 equals i mod 64. `batch`: every label occurs. `seeds`: every cluster is the seed of some cell.
All inputs are finite; a program needn't handle non-finite values.
Results may differ from a plain program's by a relative error of at most 0.012.
The roundings to bfloat16 on the way count: a program that leaves them out, or rounds other values in their place, can miss the bound.
Values may be sent and summed in bfloat16 or wider, within the bound.
No kernel may reach another device: no remote copies, remote signals or barrier semaphores. Data moves between devices by JAX's collectives and lax.ppermute only.
A program may use at most 64 MiB of HBM per device.

v0:
```python
import jax
import jax.numpy as jnp
from jax import lax
from jax.sharding import PartitionSpec as P

K = 1024
B = 64
ITERS = 2
epsilon = 1e-06
cluster_spread = 0.1


def cluster_tables(cluster_sums, observed, batch_total, total_cells):
    scaled = cluster_sums * lax.rsqrt(
        jnp.sum(cluster_sums * cluster_sums, axis=1, keepdims=True) + epsilon
    )
    cluster_mass = jnp.sum(observed, axis=1, keepdims=True)
    expected = cluster_mass * batch_total[None, :] / total_cells
    ratio = (expected + 1.0) / (observed + 1.0)
    return (scaled.astype(jnp.bfloat16), ratio * ratio)


def per_device(counts, batch, seeds, loadings):
    cell_rows = batch.shape[0]
    total_cells = cell_rows * lax.axis_size("cells") * lax.axis_size("genes")
    values = counts.astype(jnp.float32)
    depth_total = lax.psum(jnp.sum(values, axis=1), "genes")
    logged = jnp.log1p(10000.0 * values / depth_total[:, None]).astype(jnp.bfloat16)
    projected = lax.psum_scatter(
        jnp.dot(logged, loadings, preferred_element_type=jnp.float32),
        "genes",
        scatter_dimension=0,
        tiled=True,
    )
    batch_full = (batch == jnp.arange(B, dtype=jnp.int32)[None, :]).astype(jnp.float32)
    column_sum, batch_total = lax.psum(
        (jnp.sum(projected, axis=0), jnp.sum(batch_full, axis=0)), ("cells", "genes")
    )
    embedding = projected - column_sum / total_cells
    unit_rows = (
        embedding * lax.rsqrt(jnp.sum(embedding * embedding, axis=1, keepdims=True) + epsilon)
    ).astype(jnp.bfloat16)
    batch_low = batch_full.astype(jnp.bfloat16)
    assign = (seeds == jnp.arange(K, dtype=jnp.int32)[None, :]).astype(jnp.float32)
    centroids = jnp.zeros((K, unit_rows.shape[1]), jnp.bfloat16)
    leading = (((0,), (0,)), ((), ()))
    for iteration in range(ITERS):
        rounded = assign.astype(jnp.bfloat16)
        cluster_sums = lax.dot_general(
            rounded, unit_rows, leading, preferred_element_type=jnp.float32
        )
        observed = lax.dot_general(rounded, batch_low, leading, preferred_element_type=jnp.float32)
        whole_sums, whole_observed = lax.psum((cluster_sums, observed), ("cells", "genes"))
        centroids, penalty = cluster_tables(whole_sums, whole_observed, batch_total, total_cells)
        similarity = lax.dot_general(
            unit_rows, centroids, (((1,), (1,)), ((), ())), preferred_element_type=jnp.float32
        )
        distance = 2.0 - 2.0 * similarity
        lookup = lax.dot_general(
            batch_full,
            penalty,
            (((1,), (1,)), ((), ())),
            precision=lax.Precision.HIGHEST,
            preferred_element_type=jnp.float32,
        )
        weights = jnp.exp(-distance / cluster_spread) * lookup
        assign = weights / jnp.sum(weights, axis=1, keepdims=True)
    return (embedding, assign, centroids)


def solution(mesh):
    placed = (
        P("cells", "genes"),
        P(("cells", "genes"), None),
        P(("cells", "genes"), None),
        P("genes", None),
    )
    return jax.shard_map(
        per_device,
        mesh=mesh,
        in_specs=placed,
        out_specs=(P(("cells", "genes"), None), P(("cells", "genes"), None), P()),
        check_vma=False,
    )
```

profile of v0, /device:TPU:24, one launch (start us, length us, event | category | flops | bytes accessed | tf_op | source)
XLA Modules:
  0.0 763.4 jit_solution(6656614358482532397)
XLA Ops:
  7.2 1.5 convert_reduce_fusion
  8.8 32.0 %psum.49 = f32[1024]{0:T(1024)S(1)} all-reduce(f32[1024]{0:T(1024)S(1)} %convert_reduce_fusion), channel_id=1, replica_groups=mesh['cells'=32,'genes'=16] {'genes'}, use_global_device_ids=true, to_apply=%region_1.0 | all-reduce | flops 1024 | bytes 8192 | tf_op jit(solution)/shard_map/psum | solution.py:27
  40.8 1.6 fusion.9
  42.5 0.6 copy-done.10
  43.2 0.7 copy-done.9
  43.8 1.0 fusion.22
  44.8 55.2 %reduce-scatter.2.cloned.1.call-done = f32[64,256]{1,0:T(8,128)} async-done(((f32[1024,256]{1,0:T(8,128)}), f32[64,256]{1,0:T(8,128)}) %reduce-scatter.2.cloned.1.call-update) | async-done | bytes 65552 | tf_op jit(solution)/shard_map/reduce_scatter | solution.py:29
  100.0 0.9 reduce_sum.91
  101.0 96.5 %all-reduce = (f32[256]{0:T(256)S(1)}, f32[64]{0:T(128)S(1)}) all-reduce(f32[256]{0:T(256)S(1)} %reduce_sum.91, f32[64]{0:T(128)S(1)} %convert_reduce_fusion.1), channel_id=1, replica_groups=mesh['cells'=32,'genes'=16] {'cells','genes'}, use_global_device_ids=true, to_apply=%region_4.0 | all-reduce | flops 320 | bytes 2560 | tf_op jit(solution)/shard_map/psum | solution.py:36
  197.7 1.4 fusion.23
  199.2 274.5 %all-reduce.8.cloned.1.call-done = (f32[1024,256]{1,0:T(8,128)}, f32[1024,64]{0,1:T(8,128)}) async-done(((f32[1024,256]{1,0:T(8,128)}, f32[1024,64]{0,1:T(8,128)}), (f32[1024,256]{1,0:T(8,128)}, f32[1024,64]{0,1:T(8,128)})) %all-reduce.8.cloned.1.call-update) | async-done | bytes 1310736 | tf_op jit(solution)/shard_map/psum | solution.py:53
  473.7 1.5 multiply_reduce_fusion.1
  475.3 0.4 fusion.7
  475.7 0.6 copy-done.6
  476.3 0.5 fusion.45
  476.8 1.0 fusion.34
  477.8 1.4 fusion.44
  479.2 273.5 %all-reduce.6.cloned.1.call-done = (f32[1024,256]{1,0:T(8,128)}, f32[1024,64]{0,1:T(8,128)}) async-done(((f32[1024,256]{1,0:T(8,128)}, f32[1024,64]{0,1:T(8,128)}), (f32[1024,256]{1,0:T(8,128)}, f32[1024,64]{0,1:T(8,128)})) %all-reduce.6.cloned.1.call-update) | async-done | bytes 1310736 | tf_op jit(solution)/shard_map/psum | solution.py:53
  752.7 1.5 multiply_reduce_fusion
  754.3 0.2 multiply_convert_fusion
  754.5 0.7 copy-done.5
  755.2 0.3 fusion.3
  755.5 0.5 fusion.46
  756.0 0.8 broadcast_divide_fusion
  (33 shorter events, 0.6 us)
Async XLA Ops:
  7.2 33.6 %copy-start = (bf16[256,256]{1,0:T(8,128)(2,1)S(1)}, bf16[256,256]{1,0:T(8,128)(2,1)}, u32[]{:S(2)}) copy-start(bf16[256,256]{1,0:T(8,128)(2,1)} %param.7) | copy-start | bytes 393220
  7.2 33.6 %copy-start.4 = (s32[1024,256]{1,0:T(8,128)S(1)}, s32[1024,256]{1,0:T(8,128)}, u32[]{:S(2)}) copy-start(s32[1024,256]{1,0:T(8,128)} %param.4) | copy-start | bytes 3145732
  7.2 92.9 %reduce-scatter.2.cloned.1.call-start = ((), (), s32[]{:S(2)}) async-start(), calls=%async_computation.1 | async-start | bytes 1114112 | tf_op jit(solution)/shard_map/reduce_scatter | solution.py:29
  42.4 0.7 copy-start.10
  42.4 431.3 %all-reduce.8.cloned.1.call-start = ((), (), s32[]{:S(2)}) async-start(), calls=%async_computation.3 | async-start | bytes 2621440 | tf_op jit(solution)/shard_map/psum | solution.py:53
  43.2 0.7 copy-start.9
  100.0 97.4 %copy-start.8 = (f32[64,256]{1,0:T(8,128)S(1)}, f32[64,256]{1,0:T(8,128)}, u32[]{:S(2)}) copy-start(f32[64,256]{1,0:T(8,128)} %reduce-scatter.2.cloned.1.call-done) | copy-start | bytes 196612
  197.6 1.5 copy-start.7
  199.2 553.5 %all-reduce.6.cloned.1.call-start = ((), (), s32[]{:S(2)}) async-start(), calls=%async_computation.2 | async-start | bytes 2621440 | tf_op jit(solution)/shard_map/psum | solution.py:53
  473.7 1.5 copy-start.1
  475.3 1.0 copy-start.6
  752.7 1.5 copy-start.2
  754.3 1.0 copy-start.5
  754.5 1.1 copy-start.3
Sparse Core Ops, SparseCore 0:
  42.5 57.4 reduce-scatter.1
  199.3 274.4 all-reduce.7
  479.4 273.2 all-reduce.5
where the time goes:
time: 764 us; the launch traced here: 763 us
  waiting for transfers between devices  603 us (79%)
  blocking collectives  129 us (17%)
  between operations  13.9 us (2%)
  matrix products  8.11 us (1%)
    psum x2, waiting for transfers between devices, per_device(): lax.psum((cluster_sums, observed), ('cells', 'genes'))  548 us
    psum x1, blocking collectives, per_device(): lax.psum((jnp.sum(projected, axis=0), jnp.sum(batch_full, axis=0)), ('cel...  96.5 us
    reduce_scatter x1, waiting for transfers between devices, per_device(): lax.psum_scatter(jnp.dot(logged, loadings, preferred_element_type=jnp.flo...  55.2 us
    psum x1, blocking collectives, per_device(): depth_total = lax.psum(jnp.sum(values, axis=1), 'genes')  32 us
  transfers between devices with their start and end apart: 3, of which 3 were waited for; matrix products, arithmetic and copies ran while one was open for 0% of the time, Pallas kernels for 0%

commit v1 on v0

--- a/solution.py
+++ b/solution.py
@@ -24,7 +24,7 @@
     cell_rows = batch.shape[0]
     total_cells = cell_rows * lax.axis_size("cells") * lax.axis_size("genes")
     values = counts.astype(jnp.float32)
-    depth_total = lax.psum(jnp.sum(values, axis=1), "genes")
+    depth_total = jnp.sum(lax.all_gather(jnp.sum(values, axis=1), "genes"), axis=0)
     logged = jnp.log1p(10000.0 * values / depth_total[:, None]).astype(jnp.bfloat16)
     projected = lax.psum_scatter(
         jnp.dot(logged, loadings, preferred_element_type=jnp.float32),

time: 764 us -> 756 us (0.990)
  blocking collectives: 129 us -> 120 us
    psum x1 -> x0, blocking collectives: 32 us -> none  [per_device(): depth_total = lax.psum(jnp.sum(values, axis=1), 'genes')]
    all_gather x0 -> x1, blocking collectives: none -> 23.3 us  [per_device(): lax.all_gather(jnp.sum(values, axis=1), 'genes')]
where the time goes in v1:
time: 756 us
  waiting for transfers between devices  604 us (80%)
  blocking collectives  120 us (16%)
  between operations  13.9 us (2%)
  matrix products  8.1 us (1%)
    psum x2, waiting for transfers between devices, per_device(): lax.psum((cluster_sums, observed), ('cells', 'genes'))  548 us
    psum x1, blocking collectives, per_device(): lax.psum((jnp.sum(projected, axis=0), jnp.sum(batch_full, axis=0)), ('cel...  96.5 us
    reduce_scatter x1, waiting for transfers between devices, per_device(): lax.psum_scatter(jnp.dot(logged, loadings, preferred_element_type=jnp.flo...  56.3 us
    all_gather x1, blocking collectives, per_device(): lax.all_gather(jnp.sum(values, axis=1), 'genes')  23.3 us
  transfers between devices with their start and end apart: 3, of which 3 were waited for; matrix products, arithmetic and copies ran while one was open for 0% of the time, Pallas kernels for 0%

profile of v1, /device:TPU:24, one launch (start us, length us, event | category | flops | bytes accessed | tf_op | source)
XLA Modules:
  0.0 755.9 jit_solution(5789993725331986528)
XLA Ops:
  7.2 1.5 convert_reduce_fusion
  8.8 23.3 %all-gather = f32[16384]{0:T(1024)S(1)} all-gather(f32[1024]{0:T(1024)S(1)} %convert_reduce_fusion), channel_id=2, replica_groups=mesh['cells'=32,'genes'=16] {'genes'}, dimensions={0}, use_global_device_ids=true | all-gather | bytes 69632 | tf_op jit(solution)/shard_map/all_gather | solution.py:27
  32.2 1.6 fusion.9
  33.9 0.6 copy-done.10
  34.5 0.7 copy-done.9
  35.2 1.0 fusion.22
  36.2 56.3 %reduce-scatter.2.cloned.1.call-done = f32[64,256]{1,0:T(8,128)} async-done(((f32[1024,256]{1,0:T(8,128)}), f32[64,256]{1,0:T(8,128)}) %reduce-scatter.2.cloned.1.call-update) | async-done | bytes 65552 | tf_op jit(solution)/shard_map/reduce_scatter | solution.py:29
  92.5 0.9 reduce_sum.101
  93.4 96.5 %all-reduce = (f32[256]{0:T(256)S(1)}, f32[64]{0:T(128)S(1)}) all-reduce(f32[256]{0:T(256)S(1)} %reduce_sum.101, f32[64]{0:T(128)S(1)} %convert_reduce_fusion.1), channel_id=1, replica_groups=mesh['cells'=32,'genes'=16] {'cells','genes'}, use_global_device_ids=true, to_apply=%region_4.0 | all-reduce | flops 320 | bytes 2560 | tf_op jit(solution)/shard_map/psum | solution.py:36
  190.1 1.4 fusion.23
  191.7 274.6 %all-reduce.8.cloned.1.call-done = (f32[1024,256]{1,0:T(8,128)}, f32[1024,64]{0,1:T(8,128)}) async-done(((f32[1024,256]{1,0:T(8,128)}, f32[1024,64]{0,1:T(8,128)}), (f32[1024,256]{1,0:T(8,128)}, f32[1024,64]{0,1:T(8,128)})) %all-reduce.8.cloned.1.call-update) | async-done | bytes 1310736 | tf_op jit(solution)/shard_map/psum | solution.py:53
  466.3 1.5 multiply_reduce_fusion.1
  467.8 0.4 fusion.7
  468.2 0.6 copy-done.6
  468.8 0.5 fusion.45
  469.3 1.0 fusion.34
  470.3 1.4 fusion.44
  471.8 273.5 %all-reduce.6.cloned.1.call-done = (f32[1024,256]{1,0:T(8,128)}, f32[1024,64]{0,1:T(8,128)}) async-done(((f32[1024,256]{1,0:T(8,128)}, f32[1024,64]{0,1:T(8,128)}), (f32[1024,256]{1,0:T(8,128)}, f32[1024,64]{0,1:T(8,128)})) %all-reduce.6.cloned.1.call-update) | async-done | bytes 1310736 | tf_op jit(solution)/shard_map/psum | solution.py:53
  745.2 1.5 multiply_reduce_fusion
  746.8 0.2 multiply_convert_fusion
  747.0 0.7 copy-done.5
  747.8 0.3 fusion.3
  748.1 0.5 fusion.46
  748.6 0.8 broadcast_divide_fusion
  (35 shorter events, 0.6 us)
Async XLA Ops:
  7.2 25.0 %copy-start = (bf16[256,256]{1,0:T(8,128)(2,1)S(1)}, bf16[256,256]{1,0:T(8,128)(2,1)}, u32[]{:S(2)}) copy-start(bf16[256,256]{1,0:T(8,128)(2,1)} %param.7) | copy-start | bytes 393220
  7.2 25.0 %copy-start.4 = (s32[1024,256]{1,0:T(8,128)S(1)}, s32[1024,256]{1,0:T(8,128)}, u32[]{:S(2)}) copy-start(s32[1024,256]{1,0:T(8,128)} %param.4) | copy-start | bytes 3145732
  7.2 85.3 %reduce-scatter.2.cloned.1.call-start = ((), (), s32[]{:S(2)}) async-start(), calls=%async_computation.1 | async-start | bytes 1114112 | tf_op jit(solution)/shard_map/reduce_scatter | solution.py:29
  33.8 0.7 copy-start.10
  33.8 432.5 %all-reduce.8.cloned.1.call-start = ((), (), s32[]{:S(2)}) async-start(), calls=%async_computation.3 | async-start | bytes 2621440 | tf_op jit(solution)/shard_map/psum | solution.py:53
  34.5 0.7 copy-start.9
  92.5 97.5 %copy-start.8 = (f32[64,256]{1,0:T(8,128)S(1)}, f32[64,256]{1,0:T(8,128)}, u32[]{:S(2)}) copy-start(f32[64,256]{1,0:T(8,128)} %reduce-scatter.2.cloned.1.call-done) | copy-start | bytes 196612
  190.0 1.5 copy-start.7
  191.6 553.6 %all-reduce.6.cloned.1.call-start = ((), (), s32[]{:S(2)}) async-start(), calls=%async_computation.2 | async-start | bytes 2621440 | tf_op jit(solution)/shard_map/psum | solution.py:53
  466.3 1.5 copy-start.1
  467.8 1.0 copy-start.6
  745.2 1.5 copy-start.2
  746.8 1.0 copy-start.5
  747.0 1.1 copy-start.3
Sparse Core Ops, SparseCore 0:
  33.9 58.5 reduce-scatter.1
  191.7 274.4 all-reduce.7
  471.9 273.2 all-reduce.5
